TPU v7x, 32 devices: a whole 2x2x4 slice. The times are simulated.
32 devices in a mesh: shard: 4 (over z), ctx: 4 (over x, core), tp: 2 (over y).
Axes of the slice: x: 2, y: 2, z: 4, core: 2. Of those that a mesh axis runs over, the one named last changes fastest.
Arguments:
- hidden_in: bfloat16 [4, 1024, 1024], P('shard', 'ctx'), may hold values from -6 to 6
- out_grad: bfloat16 [4, 1024, 1024], P('shard', 'ctx'), may hold values from -6 to 6
- segment_ids: int32 [4, 1024], P('shard'), may hold values from 0 to 3, never falling along the last dimension, each value on 1 to 512 neighbouring positions
- w_qkv: bfloat16 [3, 1024, 1024], P(None, 'shard', 'tp'), may hold values from -0.1875 to 0.1875
- bias_qv: float32 [2, 1024], P(None, 'tp'), may hold values from -3 to 3
- w_out: bfloat16 [1024, 1024], P('tp', 'shard'), may hold values from -0.75 to 0.75
- bias_out: float32 [1024], replicated, may hold values from -3 to 3
- norm1_gain: float32 [1024], replicated, may hold values from 0.5 to 1.5
- norm1_shift: float32 [1024], replicated, may hold values from -3 to 3
- w_up: bfloat16 [1024, 4096], P('shard', 'tp'), may hold values from -0.1875 to 0.1875
- bias_up: float32 [4096], P('tp'), may hold values from -3 to 3
- w_down: bfloat16 [4096, 1024], P('tp', 'shard'), may hold values from -0.09375 to 0.09375
- bias_down: float32 [1024], replicated, may hold values from -3 to 3
- norm2_gain: float32 [1024], replicated, may hold values from 0.5 to 1.5
- norm2_shift: float32 [1024], replicated, may hold values from -3 to 3
Outputs:
- output: bfloat16 [4, 1024, 1024], P('shard', 'ctx')
- input_grad: bfloat16 [4, 1024, 1024], P('shard', 'ctx')
- w_qkv_grad: float32 [3, 1024, 1024], P(None, 'shard', 'tp')
- bias_qv_grad: float32 [2, 1024], P(None, 'tp')
- w_out_grad: float32 [1024, 1024], P('tp', 'shard')
- bias_out_grad: float32 [1024], replicated
- norm1_gain_grad: float32 [1024], replicated
- norm1_shift_grad: float32 [1024], replicated
- w_up_grad: float32 [1024, 4096], P('shard', 'tp')
- bias_up_grad: float32 [4096], P('tp')
- w_down_grad: float32 [4096, 1024], P('tp', 'shard')
- bias_down_grad: float32 [1024], replicated
- norm2_gain_grad: float32 [1024], replicated
- norm2_shift_grad: float32 [1024], replicated
Inputs may be any that keep to these rules, and one draw needn't show every extreme that they name: `segment_ids`: within each sequence the ids never fall and start at 0; each document has at most 512 tokens, and some document has exactly that many.
All inputs are finite; a program needn't handle non-finite values.
Results may differ from a plain program's by a relative error of at most 0.022.
The roundings to bfloat16 on the way count: a program that leaves them out, or rounds other values in their place, can miss the bound.
Values may be sent and summed in bfloat16 or wider, within the bound.
A program may use at most 128 MiB of HBM per device.

v0:
```python
import math
import jax
import jax.numpy as jnp
from jax import lax
from jax.sharding import PartitionSpec as P

HEADS = 16
EPSILON = 1e-05


def normalize(resid, gain, shift):
    average = jnp.mean(resid, axis=-1, keepdims=True)
    centred = resid - average
    variance = jnp.mean(centred * centred, axis=-1, keepdims=True)
    inv_std = lax.rsqrt(variance + EPSILON)
    normed = centred * inv_std
    return (normed * gain + shift, normed, inv_std)


def normalize_back(cotan, normed, inv_std, gain):
    scaled = cotan * gain
    return inv_std * (
        scaled
        - jnp.mean(scaled, axis=-1, keepdims=True)
        - normed * jnp.mean(scaled * normed, axis=-1, keepdims=True)
    )


def gelu_value(pre_act):
    return 0.5 * pre_act * (1.0 + jax.scipy.special.erf(pre_act * 0.7071067811865476))


def gelu_slope(pre_act):
    return (
        0.5 * (1.0 + jax.scipy.special.erf(pre_act * 0.7071067811865476))
        + pre_act * jnp.exp(-0.5 * pre_act * pre_act) * 0.3989422804014327
    )


def block_scores(query_block, keys, ids_block, ids_whole, scale):
    scores = (
        jnp.einsum("qhe,khe->hqk", query_block, keys, preferred_element_type=jnp.float32) * scale
    )
    return jnp.where((ids_block[:, None] == ids_whole[None, :])[None], scores, -jnp.inf)


GROUP = ("ctx", "tp")


def dot_t(left, right):
    return lax.dot_general(
        left, right, (((1,), (1,)), ((), ())), preferred_element_type=jnp.float32
    )


def dot_rows(left, right):
    return lax.dot_general(
        left, right, (((0,), (0,)), ((), ())), preferred_element_type=jnp.float32
    )


def dot(left, right):
    return jnp.dot(left, right, preferred_element_type=jnp.float32)


def spread(part):
    return lax.all_gather(part, GROUP, axis=1, tiled=True)


def collect(whole):
    return lax.psum_scatter(whole, GROUP, scatter_dimension=1, tiled=True).astype(jnp.float32)


def shards(
    hidden_in,
    out_grad,
    segment_ids,
    w_qkv,
    bias_qv,
    w_out,
    bias_out,
    norm1_gain,
    norm1_shift,
    w_up,
    bias_up,
    w_down,
    bias_down,
    norm2_gain,
    norm2_shift,
):
    seq_count, local_len, width = hidden_in.shape
    ctx_count = lax.axis_size("ctx")
    tp_count = lax.axis_size("tp")
    ctx_at = lax.axis_index("ctx")
    tp_at = lax.axis_index("tp")
    full_len = local_len * ctx_count
    part_len = local_len // tp_count
    row_count = seq_count * full_len
    head_dim = width // HEADS
    scale = 1.0 / math.sqrt(head_dim)
    owned_rows = w_up.shape[0]
    cols = w_qkv.shape[2] // ctx_count
    units = w_up.shape[1] // ctx_count
    local_heads = cols // head_dim
    block_rows = min(512, full_len)
    block_count = full_len // block_rows

    def mine(array, size, axis):
        return lax.dynamic_slice_in_dim(array, ctx_at * size, size, axis)

    qkv_own = mine(w_qkv, cols, 2).transpose(1, 0, 2).reshape(owned_rows, 3 * cols)
    qkv_full = lax.all_gather(qkv_own, "shard", axis=0, tiled=True)
    tokens_all = lax.all_gather(hidden_in, "ctx", axis=1, tiled=True).reshape(row_count, width)
    rest_own = jnp.concatenate(
        [mine(w_out, cols, 0).T, mine(w_up, units, 1), mine(w_down, units, 0).T], axis=1
    )
    rest_full = lax.all_gather(rest_own, "shard", axis=0, tiled=True)
    out_full = rest_full[:, :cols]
    up_full = rest_full[:, cols : cols + units]
    down_full = rest_full[:, cols + units :]
    bias_own = mine(bias_qv, cols, 1)
    bias_three = jnp.concatenate([bias_own[0], jnp.zeros_like(bias_own[0]), bias_own[1]])
    project = (dot(tokens_all, qkv_full) + bias_three).astype(jnp.bfloat16)
    heads = project.reshape(seq_count, full_len, 3, local_heads, head_dim)

    def attend_sequence(packed):
        seq_heads, seq_ids = packed
        keys = seq_heads[:, 1]
        values = seq_heads[:, 2]
        queries = seq_heads[:, 0].reshape(block_count, block_rows, local_heads, head_dim)
        id_blocks = seq_ids.reshape(block_count, block_rows)

        def attend_block(piece):
            query_block, ids_block = piece
            scores = block_scores(query_block, keys, ids_block, seq_ids, scale)
            log_total = jax.nn.logsumexp(scores, axis=-1)
            probs_low = jnp.exp(scores - log_total[..., None]).astype(jnp.bfloat16)
            attended = jnp.einsum(
                "hqk,khe->qhe", probs_low, values, preferred_element_type=jnp.float32
            ).astype(jnp.bfloat16)
            return (attended, log_total)

        attended, log_total = lax.map(attend_block, (queries, id_blocks))
        return (attended.reshape(full_len, local_heads, head_dim), log_total)

    attended_heads, log_totals = lax.map(attend_sequence, (heads, segment_ids))
    attended = attended_heads.reshape(row_count, cols)

    def whole(part):
        return part.astype(jnp.bfloat16).reshape(seq_count, full_len, width)

    def part_of(array):
        return lax.dynamic_slice_in_dim(array, tp_at * part_len, part_len, 1)

    resid_one = (
        collect(whole(dot_t(attended, out_full)))
        + bias_out
        + part_of(hidden_in).astype(jnp.float32)
    )
    first, normed_one, inv_one = normalize(resid_one, norm1_gain, norm1_shift)
    first_all = spread(first.astype(jnp.bfloat16)).reshape(row_count, width)
    pre_act = dot(first_all, up_full) + mine(bias_up, units, 0)
    activated = gelu_value(pre_act).astype(jnp.bfloat16)
    resid_two = collect(whole(dot_t(activated, down_full))) + bias_down + first
    result, normed_two, inv_two = normalize(resid_two, norm2_gain, norm2_shift)
    grad_float = part_of(out_grad).astype(jnp.float32)

    def total(array):
        return jnp.sum(array, axis=(0, 1))

    gain_two_grad = total(grad_float * normed_two)
    shift_two_grad = total(grad_float)
    resid_two_grad = normalize_back(grad_float, normed_two, inv_two, norm2_gain)
    two_all = spread(resid_two_grad.astype(jnp.bfloat16)).reshape(row_count, width)
    output = lax.all_gather(result.astype(jnp.bfloat16), "tp", axis=1, tiled=True)
    bias_down_grad = total(resid_two_grad)
    pre_grad = dot(two_all, down_full) * gelu_slope(pre_act)
    pre_low = pre_grad.astype(jnp.bfloat16)
    bias_up_grad = jnp.sum(pre_grad, axis=0)
    first_grad = resid_two_grad + collect(whole(dot_t(pre_low, up_full)))
    part_ffn = jnp.concatenate(
        [dot_rows(first_all, pre_low), dot_rows(two_all, activated)], axis=1
    ).astype(jnp.bfloat16)
    gain_one_grad = total(first_grad * normed_one)
    shift_one_grad = total(first_grad)
    resid_one_grad = normalize_back(first_grad, normed_one, inv_one, norm1_gain)
    bias_out_grad = total(resid_one_grad)
    one_all = spread(resid_one_grad.astype(jnp.bfloat16)).reshape(row_count, width)
    attended_grad = dot(one_all, out_full).astype(jnp.bfloat16)
    grad_heads = attended_grad.reshape(seq_count, full_len, local_heads, head_dim)

    def back_sequence(packed):
        seq_heads, seq_ids, seq_attended, seq_grad, seq_log = packed
        keys = seq_heads[:, 1]
        values = seq_heads[:, 2]
        queries = seq_heads[:, 0].reshape(block_count, block_rows, local_heads, head_dim)
        id_blocks = seq_ids.reshape(block_count, block_rows)
        att_blocks = seq_attended.reshape(block_count, block_rows, local_heads, head_dim)
        grad_blocks = seq_grad.reshape(block_count, block_rows, local_heads, head_dim)

        def back_block(carry, piece):
            key_total, value_total = carry
            query_block, ids_block, att_block, grad_block, log_block = piece
            scores = block_scores(query_block, keys, ids_block, seq_ids, scale)
            probs = jnp.exp(scores - log_block[..., None])
            probs_low = probs.astype(jnp.bfloat16)
            prob_grad = jnp.einsum(
                "qhe,khe->hqk", grad_block, values, preferred_element_type=jnp.float32
            )
            offset = jnp.sum(
                grad_block.astype(jnp.float32) * att_block.astype(jnp.float32), axis=-1
            ).T
            score_grad = (probs * (prob_grad - offset[..., None]) * scale).astype(jnp.bfloat16)
            query_grad = jnp.einsum(
                "hqk,khe->qhe", score_grad, keys, preferred_element_type=jnp.float32
            ).astype(jnp.bfloat16)
            key_total = key_total + jnp.einsum(
                "hqk,qhe->khe", score_grad, query_block, preferred_element_type=jnp.float32
            )
            value_total = value_total + jnp.einsum(
                "hqk,qhe->khe", probs_low, grad_block, preferred_element_type=jnp.float32
            )
            return ((key_total, value_total), query_grad)

        empty = jnp.zeros((full_len, local_heads, head_dim), jnp.float32)
        (key_total, value_total), query_grads = lax.scan(
            back_block, (empty, empty), (queries, id_blocks, att_blocks, grad_blocks, seq_log)
        )
        return jnp.stack(
            [
                query_grads.reshape(full_len, local_heads, head_dim),
                key_total.astype(jnp.bfloat16),
                value_total.astype(jnp.bfloat16),
            ],
            axis=1,
        )

    head_grads = lax.map(
        back_sequence, (heads, segment_ids, attended_heads, grad_heads, log_totals)
    )
    proj_grad = head_grads.reshape(row_count, 3 * cols)
    proj_sum = jnp.sum(proj_grad.astype(jnp.float32), axis=0)
    bias_qv_grad = jnp.concatenate([proj_sum[:cols], proj_sum[2 * cols :]])
    input_part = resid_one_grad + collect(whole(dot_t(proj_grad, qkv_full)))
    input_grad = lax.all_gather(input_part.astype(jnp.bfloat16), "tp", axis=1, tiled=True)
    part_attn = jnp.concatenate(
        [dot_rows(tokens_all, proj_grad), dot_rows(one_all, attended)], axis=1
    ).astype(jnp.bfloat16)

    def owned(part):
        mean = lax.psum_scatter(part, "shard", scatter_dimension=0, tiled=True)
        return lax.all_gather(mean, "ctx", axis=0).astype(jnp.float32)

    own_ffn = owned(part_ffn)
    own_attn = owned(part_attn)
    up_grad = own_ffn[:, :, :units].transpose(1, 0, 2).reshape(w_up.shape)
    down_grad = own_ffn[:, :, units:].transpose(0, 2, 1).reshape(w_down.shape)
    qkv_grad = (
        own_attn[:, :, : 3 * cols]
        .reshape(ctx_count, owned_rows, 3, cols)
        .transpose(2, 1, 0, 3)
        .reshape(w_qkv.shape)
    )
    out_weight_grad = own_attn[:, :, 3 * cols :].transpose(0, 2, 1).reshape(w_out.shape)
    sliced = jnp.concatenate([bias_qv_grad, bias_up_grad])
    slots = jnp.zeros((tp_count, ctx_count, sliced.shape[0]), jnp.float32)
    slots = lax.dynamic_update_slice(slots, sliced[None, None], (tp_at, ctx_at, 0))
    small = lax.psum(
        jnp.concatenate(
            [
                bias_out_grad,
                gain_one_grad,
                shift_one_grad,
                bias_down_grad,
                gain_two_grad,
                shift_two_grad,
                slots.reshape(-1),
            ]
        ),
        ("shard", "ctx", "tp"),
    )
    sums = small[: 6 * width].reshape(6, width)
    slots = small[6 * width :].reshape(tp_count, ctx_count, -1)
    slots = lax.dynamic_index_in_dim(slots, tp_at, 0, keepdims=False)
    bias_qv_total = (
        slots[:, : 2 * cols].reshape(ctx_count, 2, cols).transpose(1, 0, 2).reshape(bias_qv.shape)
    )
    return (
        output,
        input_grad,
        qkv_grad,
        bias_qv_total,
        out_weight_grad,
        sums[0],
        sums[1],
        sums[2],
        up_grad,
        slots[:, 2 * cols :].reshape(bias_up.shape),
        down_grad,
        sums[3],
        sums[4],
        sums[5],
    )


def solution(mesh):
    return jax.shard_map(
        shards,
        mesh=mesh,
        in_specs=(
            P("shard", "ctx", None),
            P("shard", "ctx", None),
            P("shard", None),
            P(None, "shard", "tp"),
            P(None, "tp"),
            P("tp", "shard"),
            P(),
            P(),
            P(),
            P("shard", "tp"),
            P("tp"),
            P("tp", "shard"),
            P(),
            P(),
            P(),
        ),
        out_specs=(
            P("shard", "ctx", None),
            P("shard", "ctx", None),
            P(None, "shard", "tp"),
            P(None, "tp"),
            P("tp", "shard"),
            P(),
            P(),
            P(),
            P("shard", "tp"),
            P("tp"),
            P("tp", "shard"),
            P(),
            P(),
            P(),
        ),
        check_vma=False,
    )
```

profile of v0, /device:TPU:0, one launch (start us, length us, event | category | flops | bytes accessed | tf_op | source)
XLA Modules:
  0.0 506.4 jit_solution(6332370861797403989)
XLA Ops:
  14.3 21.3 %all_gather.36 = bf16[1024,384]{0,1:T(8,128)(2,1)S(1)} all-gather(bf16[256,384]{0,1:T(8,128)(2,1)S(1)} %bitcast.238), channel_id=1, replica_groups=mesh['shard'=4,'ctx'=4,'tp'=2] {'shard'}, dimensions={0}, use_global_device_ids=true | all-gather | bytes 983040 | tf_op jit(solution)/shard_map/all_gather | solution.py:112
  35.7 2.6 add_convert_fusion
  38.6 7.9 %while.45 = (s32[]{:T(128)}, bf16[2,512,2,64]{1,3,2,0:T(8,128)(2,1)S(1)}, f32[2,2,512]{2,1,0:T(2,128)S(1)}, s32[2,512]{1,0:T(2,128)S(1)}, s32[1024]{0:T(1024)S(1...) while((s32[]{:T(128)}, ...), condition=%wide.region_3.4_spmd, body=%wide.region_0.3_spmd.sunk | while | flops 280567808 | bytes 15526005 | solution.py:143
  46.8 40.8 %all-gather.12.cloned.1.call-done = bf16[1024,1152]{0,1:T(8,128)(2,1)} async-done(((bf16[256,1152]{0,1:T(8,128)(2,1)}), bf16[1024,1152]{0,1:T(8,128)(2,1)}) %all-gather.12.cloned.1.call-update) | async-done | bytes 2359312 | tf_op jit(solution)/shard_map/all_gather | solution.py:117
  87.6 3.1 convert_bitcast_fusion.3
  90.8 40.0 %reduce-scatter.7.cloned.1.call-done = bf16[1,128,1024]{2,1,0:T(8,128)(2,1)} async-done(((bf16[1,1024,1024]{2,1,0:T(8,128)(2,1)}), bf16[1,128,1024]{2,1,0:T(8,128)(2,1)}) %reduce-scatter.7.cloned.1.call-update) | async-done | bytes 262160 | tf_op jit(solution)/shard_map/reduce_scatter | solution.py:71
  135.8 27.1 %all-gather.14.cloned.1.call-done = bf16[1,1024,1024]{2,1,0:T(8,128)(2,1)} async-done(((bf16[1,128,1024]{2,1,0:T(8,128)(2,1)}), bf16[1,1024,1024]{2,1,0:T(8,128)(2,1)}) %all-gather.14.cloned.1.call-update) | async-done | bytes 2097168 | tf_op jit(solution)/shard_map/all_gather | solution.py:67
  162.9 4.6 multiply_convert_fusion.1
  168.4 3.8 convert_bitcast_fusion.2
  172.3 41.2 %reduce-scatter.9.cloned.1.call-done = bf16[1,128,1024]{2,1,0:T(8,128)(2,1)} async-done(((bf16[1,1024,1024]{2,1,0:T(8,128)(2,1)}), bf16[1,128,1024]{2,1,0:T(8,128)(2,1)}) %reduce-scatter.9.cloned.1.call-update) | async-done | bytes 262160 | tf_op jit(solution)/shard_map/reduce_scatter | solution.py:71
  216.6 27.7 %all-gather.16.cloned.1.call-done = bf16[1,1024,1024]{2,1,0:T(8,128)(2,1)} async-done(((bf16[1,128,1024]{2,1,0:T(8,128)(2,1)}), bf16[1,1024,1024]{2,1,0:T(8,128)(2,1)}) %all-gather.16.cloned.1.call-update) | async-done | bytes 2097168 | tf_op jit(solution)/shard_map/all_gather | solution.py:67
  244.3 4.5 fusion.111
  249.8 3.8 convert_bitcast_fusion.1
  253.7 41.2 %reduce-scatter.11.cloned.1.call-done = bf16[1,128,1024]{2,1,0:T(8,128)(2,1)} async-done(((bf16[1,1024,1024]{2,1,0:T(8,128)(2,1)}), bf16[1,128,1024]{2,1,0:T(8,128)(2,1)}) %reduce-scatter.11.cloned.1.call-update) | async-done | bytes 262160 | tf_op jit(solution)/shard_map/reduce_scatter | solution.py:71
  299.1 3.3 fusion.72
  305.5 21.4 %all-gather.18.cloned.1.call-done = bf16[1,1024,1024]{2,1,0:T(8,128)(2,1)} async-done(((bf16[1,128,1024]{2,1,0:T(8,128)(2,1)}), bf16[1,1024,1024]{2,1,0:T(8,128)(2,1)}) %all-gather.18.cloned.1.call-update) | async-done | bytes 2097168 | tf_op jit(solution)/shard_map/all_gather | solution.py:67
  326.9 2.3 fusion.81
  329.9 12.5 %while.46 = (s32[]{:T(128)}, f32[1024,2,64]{0,2,1:T(8,128)S(1)}, f32[1024,2,64]{0,2,1:T(8,128)}, bf16[2,512,2,64]{1,3,2,0:T(8,128)(2,1)S(1)}, bf16[2,512,2,64]{1...) while((s32[]{:T(128)}, f32[1024,2,64]{0,2,1:T(8,128)S(1)}, ...), condition=%wide.region_17.18_spmd.clone, body=%wide.region_15.17_spmd.clone.sunk | while | flops 683998208 | bytes 29526284 | solution.py:226
  344.2 2.2 fusion.84
  348.4 25.0 %reduce-scatter.17.cloned.1.call-done = bf16[256,1024]{0,1:T(8,128)(2,1)} async-done(((bf16[1024,1024]{0,1:T(8,128)(2,1)}), bf16[256,1024]{0,1:T(8,128)(2,1)}) %reduce-scatter.17.cloned.1.call-update) | async-done | bytes 524304 | tf_op jit(solution)/shard_map/reduce_scatter | solution.py:251
  373.5 2.6 convert_bitcast_fusion
  376.2 8.4 %all_gather.40 = bf16[1,256,1024]{2,1,0:T(8,128)(2,1)} all-gather(bf16[1,128,1024]{2,1,0:T(8,128)(2,1)S(1)} %get-tuple-element.297), channel_id=1, replica_groups=mesh['shard'=4,'ctx'=4,'tp'=2] {'tp'}, dimensions={1}, use_global_device_ids=true | all-gather | bytes 786432 | tf_op jit(solution)/shard_map/all_gather | solution.py:175
  385.0 17.8 %reduce-scatter.15.cloned.1.call-done = bf16[256,512]{0,1:T(8,128)(2,1)} async-done(((bf16[1024,512]{0,1:T(8,128)(2,1)}), bf16[256,512]{0,1:T(8,128)(2,1)}) %reduce-scatter.15.cloned.1.call-update) | async-done | bytes 262160 | tf_op jit(solution)/shard_map/reduce_scatter | solution.py:251
  402.8 39.6 %psum.7 = f32[12288]{0:T(1024)S(1)} all-reduce(f32[12288]{0:T(1024)S(1)} %constant_dynamic-update-slice_fusion), channel_id=1, replica_groups=mesh['shard'=4,'ctx'=4,'tp'=2] {'shard','ctx','tp'}, use_global_device_ids=true, to_apply=%region_28.29 | all-reduce | flops 12288 | bytes 98304 | tf_op jit(solution)/shard_map/psum | solution.py:268
  444.3 5.0 reshape.372
  449.3 4.5 slice_bitcast_fusion
  455.5 2.9 copy.45
  458.4 2.2 copy.53
  460.6 9.5 %reduce-scatter.13.cloned.1.call-done = bf16[1,128,1024]{2,1,0:T(8,128)(2,1)} async-done(((bf16[1,1024,1024]{2,1,0:T(8,128)(2,1)}), bf16[1,128,1024]{2,1,0:T(8,128)(2,1)}) %reduce-scatter.13.cloned.1.call-update) | async-done | bytes 262160 | tf_op jit(solution)/shard_map/reduce_scatter | solution.py:71
  471.1 8.6 %all_gather.43 = bf16[1,256,1024]{2,1,0:T(8,128)(2,1)} all-gather(bf16[1,128,1024]{2,1,0:T(8,128)(2,1)S(1)} %add_convert_fusion.1), channel_id=1, replica_groups=mesh['shard'=4,'ctx'=4,'tp'=2] {'tp'}, dimensions={1}, use_global_device_ids=true | all-gather | bytes 786432 | tf_op jit(solution)/shard_map/all_gather | solution.py:245
  479.7 8.7 %all-gather.20.cloned.1.call-done = bf16[1024,512]{0,1:T(8,128)(2,1)} async-done(((bf16[256,512]{0,1:T(8,128)(2,1)}), bf16[1024,512]{0,1:T(8,128)(2,1)}) %all-gather.20.cloned.1.call-update) | async-done | bytes 1048592 | tf_op jit(solution)/shard_map/all_gather | solution.py:252
  496.3 2.0 copy.44
  (205 shorter events, 63.9 us)
Async XLA Ops:
  7.2 5.3 %copy-start.12 = (s32[1,1024]{1,0:T(1,128)S(1)}, s32[1,1024]{1,0:T(1,128)}, u32[]{:S(2)}) copy-start(s32[1,1024]{1,0:T(1,128)} %param.21) | copy-start | bytes 12292
  7.2 28.5 %all-gather.10.cloned.1.call-start = ((), (), s32[]{:S(2)}) async-start(), calls=%async_computation.6 | async-start | bytes 2621440 | tf_op jit(solution)/shard_map/all_gather | solution.py:113
  7.9 79.7 %all-gather.12.cloned.1.call-start = ((), (), s32[]{:S(2)}) async-start(), calls=%async_computation.7 | async-start | bytes 2949120 | tf_op jit(solution)/shard_map/all_gather | solution.py:117
  11.3 119.5 %reduce-scatter.7.cloned.1.call-start = ((), (), s32[]{:S(2)}) async-start(), calls=%async_computation.8 | async-start | bytes 2359296 | tf_op jit(solution)/shard_map/reduce_scatter | solution.py:71
  46.5 44.2 %copy-start.13 = (bf16[1024,2,64]{0,2,1:T(8,128)(2,1)}, bf16[1024,2,64]{0,2,1:T(8,128)(2,1)S(1)}, u32[]{:S(2)}) copy-start(bf16[1024,2,64]{0,2,1:T(8,128)(2,1)S(1)} %get-tuple-element.588) | copy-start | bytes 786436
  87.6 43.2 %copy-start.3 = (bf16[1,256,1024]{2,1,0:T(8,128)(2,1)S(1)}, bf16[1,256,1024]{2,1,0:T(8,128)(2,1)}, u32[]{:S(2)}) copy-start(bf16[1,256,1024]{2,1,0:T(8,128)(2,1)} %param.19) | copy-start | bytes 1572868
  87.6 43.2 %copy-start.15 = (f32[1024]{0:T(1024)S(1)}, f32[1024]{0:T(1024)}, u32[]{:S(2)}) copy-start(f32[1024]{0:T(1024)} %param.25) | copy-start | bytes 12292
  90.7 42.4 %copy-start.16 = (f32[1024]{0:T(1024)S(1)}, f32[1024]{0:T(1024)}, u32[]{:S(2)}) copy-start(f32[1024]{0:T(1024)} %param.26) | copy-start | bytes 12292
  90.7 42.4 %copy-start.17 = (f32[1024]{0:T(1024)S(1)}, f32[1024]{0:T(1024)}, u32[]{:S(2)}) copy-start(f32[1024]{0:T(1024)} %param.27) | copy-start | bytes 12292
  90.7 72.2 %all-gather.14.cloned.1.call-start = ((), (), s32[]{:S(2)}) async-start(), calls=%async_computation.9 | async-start | bytes 2359296 | tf_op jit(solution)/shard_map/all_gather | solution.py:67
  134.9 78.6 %reduce-scatter.9.cloned.1.call-start = ((), (), s32[]{:S(2)}) async-start(), calls=%async_computation.10 | async-start | bytes 2359296 | tf_op jit(solution)/shard_map/reduce_scatter | solution.py:71
  172.2 41.3 %copy-start.2 = (bf16[1,128,1024]{2,1,0:T(8,128)(2,1)S(1)}, bf16[1,128,1024]{2,1,0:T(8,128)(2,1)}, u32[]{:S(2)}) copy-start(bf16[1,128,1024]{2,1,0:T(8,128)(2,1)} %reduce-scatter.7.cloned.1.call-done) | copy-start | bytes 786436
  172.2 41.3 %copy-start.19 = (f32[1024]{0:T(1024)S(1)}, f32[1024]{0:T(1024)}, u32[]{:S(2)}) copy-start(f32[1024]{0:T(1024)} %param.31) | copy-start | bytes 12292
  172.2 42.8 %copy-start.10 = (bf16[1,256,1024]{2,1,0:T(8,128)(2,1)S(1)}, bf16[1,256,1024]{2,1,0:T(8,128)(2,1)}, u32[]{:S(2)}) copy-start(bf16[1,256,1024]{2,1,0:T(8,128)(2,1)} %param.20) | copy-start | bytes 1572868
  172.2 42.8 %copy-start.18 = (f32[1024]{0:T(1024)S(1)}, f32[1024]{0:T(1024)}, u32[]{:S(2)}) copy-start(f32[1024]{0:T(1024)} %param.32) | copy-start | bytes 12292
  172.2 43.1 %copy-start.20 = (f32[1024]{0:T(1024)S(1)}, f32[1024]{0:T(1024)}, u32[]{:S(2)}) copy-start(f32[1024]{0:T(1024)} %param.33) | copy-start | bytes 12292
  172.3 72.0 %all-gather.16.cloned.1.call-start = ((), (), s32[]{:S(2)}) async-start(), calls=%async_computation.11 | async-start | bytes 2359296 | tf_op jit(solution)/shard_map/all_gather | solution.py:67
  216.4 78.5 %reduce-scatter.11.cloned.1.call-start = ((), (), s32[]{:S(2)}) async-start(), calls=%async_computation.12 | async-start | bytes 2359296 | tf_op jit(solution)/shard_map/reduce_scatter | solution.py:71
  253.6 73.3 %all-gather.18.cloned.1.call-start = ((), (), s32[]{:S(2)}) async-start(), calls=%async_computation.13 | async-start | bytes 2359296 | tf_op jit(solution)/shard_map/all_gather | solution.py:67
  299.0 74.5 %reduce-scatter.17.cloned.1.call-start = ((), (), s32[]{:S(2)}) async-start(), calls=%async_computation.16 | async-start | bytes 2621440 | tf_op jit(solution)/shard_map/reduce_scatter | solution.py:251
  299.1 3.3 copy-start.22
  299.1 3.3 copy-start.25
  305.3 97.5 %reduce-scatter.15.cloned.1.call-start = ((), (), s32[]{:S(2)}) async-start(), calls=%async_computation.15 | async-start | bytes 1310720 | tf_op jit(solution)/shard_map/reduce_scatter | solution.py:251
  332.8 2.0 copy-start.9
  344.0 2.4 copy-start.21
  348.4 95.9 %all-gather.22.cloned.1.call-start = ((), (), s32[]{:S(2)}) async-start(), calls=%async_computation.18 | async-start | bytes 2621440 | tf_op jit(solution)/shard_map/all_gather | solution.py:252
  373.5 96.6 %reduce-scatter.13.cloned.1.call-start = ((), (), s32[]{:S(2)}) async-start(), calls=%async_computation.14 | async-start | bytes 2359296 | tf_op jit(solution)/shard_map/reduce_scatter | solution.py:71
  376.2 112.3 %all-gather.20.cloned.1.call-start = ((), (), s32[]{:S(2)}) async-start(), calls=%async_computation.17 | async-start | bytes 1310720 | tf_op jit(solution)/shard_map/all_gather | solution.py:252
  458.4 11.7 %copy-start.5 = (f32[1,128,1024]{2,1,0:T(8,128)S(1)}, f32[1,128,1024]{2,1,0:T(8,128)}, u32[]{:S(2)}) copy-start(f32[1,128,1024]{2,1,0:T(8,128)} %copy-done.4) | copy-start | bytes 1572868
  494.5 3.8 copy-start.6
  494.5 5.4 %copy-start.1 = (bf16[256,2048]{1,0:T(8,128)(2,1)S(1)}, bf16[256,2048]{1,0:T(8,128)(2,1)}, u32[]{:S(2)}) copy-start(bf16[256,2048]{1,0:T(8,128)(2,1)} %param.28) | copy-start | bytes 3145732
  496.3 2.8 copy-start.7
  (10 other events, 12.7 us)
Sparse Core Ops, SparseCore 0:
  9.6 25.2 all-gather.9
  37.0 50.5 all-gather.11
  91.5 39.2 reduce-scatter.6
  135.1 27.7 all-gather.13
  172.4 41.0 reduce-scatter.8
  216.5 27.7 all-gather.15
  253.7 41.0 reduce-scatter.10
  299.1 27.7 all-gather.17
  329.8 43.6 reduce-scatter.16
  376.2 26.4 reduce-scatter.14
  404.3 21.4 all-gather.21
  428.9 41.1 reduce-scatter.12
  471.6 16.7 all-gather.19
where the time goes:
time: 507 us; the launch traced here: 506 us
  waiting for transfers between devices  301 us (59%)
  blocking collectives  78 us (15%)
  matrix products  50.5 us (10%)
  local copies, waits for them, and re-layouts  40.4 us (8%)
  other arithmetic  20.5 us (4%)
  between operations  14.5 us (3%)
    reduce_scatter x4, waiting for transfers between devices, collect(): lax.psum_scatter(whole, GROUP, scatter_dimension=1, tiled=True)  132 us
    all_gather x3, waiting for transfers between devices, spread(): return lax.all_gather(part, GROUP, axis=1, tiled=True)  76.2 us
    reduce_scatter x2, waiting for transfers between devices, owned(): mean = lax.psum_scatter(part, 'shard', scatter_dimension=0, tiled=True)  42.8 us
    all_gather x1, waiting for transfers between devices, shards(): rest_full = lax.all_gather(rest_own, 'shard', axis=0, tiled=True)  40.8 us
    psum x1, blocking collectives, shards(): lax.psum(jnp.concatenate([bias_out_grad, gain_one_grad, shift_one_grad, b...  39.6 us
    all_gather x1, blocking collectives, shards(): qkv_full = lax.all_gather(qkv_own, 'shard', axis=0, tiled=True)  21.3 us
    dot_general x4, matrix products, dot(): return jnp.dot(left, right, preferred_element_type=jnp.float32)  14 us
    dot_general x4, matrix products, dot_t(): lax.dot_general(left, right, (((1,), (1,)), ((), ())), preferred_element_...  13.3 us
  transfers between devices with their start and end apart: 13, of which 11 were waited for; matrix products, arithmetic and copies ran while one was open for 13% of the time, Pallas kernels for 0%

commit v1 on v0

--- a/solution.py
+++ b/solution.py
@@ -6,6 +6,24 @@
 
 HEADS = 16
 EPSILON = 1e-05
+
+
+def joined_along(blocks, dim):
+    blocks = jnp.moveaxis(blocks, 0, dim)
+    shape = blocks.shape
+    return blocks.reshape(*shape[:dim], shape[dim] * shape[dim + 1], *shape[dim + 2 :])
+
+
+def collected_by_bits(x, axis):
+    size = lax.axis_size(axis)
+    pieces = x[None]
+    for level in range(size.bit_length() - 1):
+        bit = 1 << level
+        theirs = lax.ppermute(pieces, axis, [(i, i ^ bit) for i in range(size)])
+        both = jnp.stack([pieces, theirs])
+        upper = lax.axis_index(axis) >> level & 1
+        pieces = jnp.where(upper == 0, both, both[::-1]).reshape(-1, *x.shape)
+    return pieces
 
 
 def normalize(resid, gain, shift):
@@ -114,7 +132,7 @@
     rest_own = jnp.concatenate(
         [mine(w_out, cols, 0).T, mine(w_up, units, 1), mine(w_down, units, 0).T], axis=1
     )
-    rest_full = lax.all_gather(rest_own, "shard", axis=0, tiled=True)
+    rest_full = joined_along(collected_by_bits(rest_own, "shard"), 0)
     out_full = rest_full[:, :cols]
     up_full = rest_full[:, cols : cols + units]
     down_full = rest_full[:, cols + units :]

time: 507 us -> 530 us (1.045)
  blocking collectives: 78 us -> 120 us
  waiting for transfers between devices: 301 us -> 275 us
  starting transfers between devices: 0.93 us -> 6.61 us
    all_gather x1, blocking collectives: 21.3 us -> 63.3 us  [shards(): qkv_full = lax.all_gather(qkv_own, 'shard', axis=0, tiled=True)]
    all_gather x1 -> x0, waiting for transfers between devices: 40.8 us -> none  [shards(): rest_full = lax.all_gather(rest_own, 'shard', axis=0, tiled=True)]
    ppermute x0 -> x2, waiting for transfers between devices: none -> 13.2 us  [collected_by_bits(): theirs = lax.ppermute(pieces, axis, [(i, i ^ bit) for i in range(size)])]
    ppermute x0 -> x2, starting transfers between devices: none -> 5.94 us  [collected_by_bits(): theirs = lax.ppermute(pieces, axis, [(i, i ^ bit) for i in range(size)])]
  transfers between devices with their start and end apart: 13 -> 14, of which waited for: 11 -> 11; matrix products, arithmetic and copies ran while one was open for 13% -> 11% of each run, Pallas kernels for 0% -> 0%
where the time goes in v1:
time: 530 us; the launch traced here: 529 us
  waiting for transfers between devices  275 us (52%)
  blocking collectives  120 us (23%)
  matrix products  50.6 us (10%)
  local copies, waits for them, and re-layouts  39.8 us (8%)
  other arithmetic  22.7 us (4%)
  between operations  14.8 us (3%)
  starting transfers between devices  6.61 us (1%)
    reduce_scatter x4, waiting for transfers between devices, collect(): lax.psum_scatter(whole, GROUP, scatter_dimension=1, tiled=True)  132 us
    all_gather x3, waiting for transfers between devices, spread(): return lax.all_gather(part, GROUP, axis=1, tiled=True)  76.4 us
    all_gather x1, blocking collectives, shards(): qkv_full = lax.all_gather(qkv_own, 'shard', axis=0, tiled=True)  63.3 us
    reduce_scatter x2, waiting for transfers between devices, owned(): mean = lax.psum_scatter(part, 'shard', scatter_dimension=0, tiled=True)  44.5 us
    psum x1, blocking collectives, shards(): lax.psum(jnp.concatenate([bias_out_grad, gain_one_grad, shift_one_grad, b...  39.4 us
    dot_general x4, matrix products, dot(): return jnp.dot(left, right, preferred_element_type=jnp.float32)  13.9 us
    dot_general x4, matrix products, dot_t(): lax.dot_general(left, right, (((1,), (1,)), ((), ())), preferred_element_...  13.4 us
    ppermute x2, waiting for transfers between devices, collected_by_bits(): theirs = lax.ppermute(pieces, axis, [(i, i ^ bit) for i in range(size)])  13.2 us
  transfers between devices with their start and end apart: 14, of which 11 were waited for; matrix products, arithmetic and copies ran while one was open for 11% of the time, Pallas kernels for 0%

profile of v1, /device:TPU:0, one launch (start us, length us, event | category | flops | bytes accessed | tf_op | source)
XLA Modules:
  0.0 529.1 jit_solution(11049762568703537847)
XLA Ops:
  9.7 3.1 collective-permute-start
  12.9 13.2 %collective-permute-done = bf16[1,256,1152]{2,1,0:T(8,128)(2,1)S(1)} collective-permute-done((bf16[1,256,1152]{2,1,0:T(8,128)(2,1)S(1)}, bf16[1,256,1152]{2,1,0:T(8,128)(2,1)S(1)}, u32[]{:S(2)}, u32[]{:S(2)}) %collective-permute-start) | collective-permute-done | bytes 589856 | tf_op jit(solution)/shard_map/ppermute | solution.py:22
  26.5 2.8 collective-permute-start.1
  32.3 63.3 %all_gather.33 = bf16[1024,384]{0,1:T(8,128)(2,1)S(1)} all-gather(bf16[256,384]{0,1:T(8,128)(2,1)S(1)} %bitcast.256), channel_id=1, replica_groups=mesh['shard'=4,'ctx'=4,'tp'=2] {'shard'}, dimensions={0}, use_global_device_ids=true | all-gather | bytes 983040 | tf_op jit(solution)/shard_map/all_gather | solution.py:130
  99.3 2.6 add_convert_fusion
  102.2 7.9 %while.45 = (s32[]{:T(128)}, bf16[2,512,2,64]{1,3,2,0:T(8,128)(2,1)S(1)}, f32[2,2,512]{2,1,0:T(2,128)S(1)}, s32[2,512]{1,0:T(2,128)S(1)}, s32[1024]{0:T(1024)S(1...) while((s32[]{:T(128)}, ...), condition=%wide.region_3.4_spmd, body=%wide.region_0.3_spmd.sunk | while | flops 280567808 | bytes 15526005 | solution.py:161
  110.5 3.1 convert_bitcast_fusion.3
  113.6 39.6 %reduce-scatter.7.cloned.1.call-done = bf16[1,128,1024]{2,1,0:T(8,128)(2,1)} async-done(((bf16[1,1024,1024]{2,1,0:T(8,128)(2,1)}), bf16[1,128,1024]{2,1,0:T(8,128)(2,1)}) %reduce-scatter.7.cloned.1.call-update) | async-done | bytes 262160 | tf_op jit(solution)/shard_map/reduce_scatter | solution.py:89
  158.2 27.1 %all-gather.11.cloned.1.call-done = bf16[1,1024,1024]{2,1,0:T(8,128)(2,1)} async-done(((bf16[1,128,1024]{2,1,0:T(8,128)(2,1)}), bf16[1,1024,1024]{2,1,0:T(8,128)(2,1)}) %all-gather.11.cloned.1.call-update) | async-done | bytes 2097168 | tf_op jit(solution)/shard_map/all_gather | solution.py:85
  185.3 4.5 multiply_convert_fusion.1
  190.8 3.8 convert_bitcast_fusion.2
  194.8 41.2 %reduce-scatter.9.cloned.1.call-done = bf16[1,128,1024]{2,1,0:T(8,128)(2,1)} async-done(((bf16[1,1024,1024]{2,1,0:T(8,128)(2,1)}), bf16[1,128,1024]{2,1,0:T(8,128)(2,1)}) %reduce-scatter.9.cloned.1.call-update) | async-done | bytes 262160 | tf_op jit(solution)/shard_map/reduce_scatter | solution.py:89
  239.0 27.7 %all-gather.13.cloned.1.call-done = bf16[1,1024,1024]{2,1,0:T(8,128)(2,1)} async-done(((bf16[1,128,1024]{2,1,0:T(8,128)(2,1)}), bf16[1,1024,1024]{2,1,0:T(8,128)(2,1)}) %all-gather.13.cloned.1.call-update) | async-done | bytes 2097168 | tf_op jit(solution)/shard_map/all_gather | solution.py:85
  266.7 4.5 fusion.115
  272.2 3.8 convert_bitcast_fusion.1
  276.1 41.2 %reduce-scatter.11.cloned.1.call-done = bf16[1,128,1024]{2,1,0:T(8,128)(2,1)} async-done(((bf16[1,1024,1024]{2,1,0:T(8,128)(2,1)}), bf16[1,128,1024]{2,1,0:T(8,128)(2,1)}) %reduce-scatter.11.cloned.1.call-update) | async-done | bytes 262160 | tf_op jit(solution)/shard_map/reduce_scatter | solution.py:89
  321.5 3.3 fusion.72
  327.7 21.6 %all-gather.15.cloned.1.call-done = bf16[1,1024,1024]{2,1,0:T(8,128)(2,1)} async-done(((bf16[1,128,1024]{2,1,0:T(8,128)(2,1)}), bf16[1,1024,1024]{2,1,0:T(8,128)(2,1)}) %all-gather.15.cloned.1.call-update) | async-done | bytes 2097168 | tf_op jit(solution)/shard_map/all_gather | solution.py:85
  349.3 2.3 fusion.81
  352.3 11.8 %while.46 = (s32[]{:T(128)}, f32[1024,2,64]{0,2,1:T(8,128)S(1)}, f32[1024,2,64]{0,2,1:T(8,128)S(1)}, bf16[2,512,2,64]{1,3,2,0:T(8,128)(2,1)S(1)}, bf16[2,512,2,6...) while((s32[]{:T(128)}, f32[1024,2,64]{0,2,1:T(8,128)S(1)}, ...), condition=%wide.region_17.18_spmd.clone, body=%wide.region_15.17_spmd.clone.sunk | while | flops 683998208 | bytes 24283320 | solution.py:244
  369.2 26.7 %reduce-scatter.17.cloned.1.call-done = bf16[256,1024]{0,1:T(8,128)(2,1)} async-done(((bf16[1024,1024]{0,1:T(8,128)(2,1)}), bf16[256,1024]{0,1:T(8,128)(2,1)}) %reduce-scatter.17.cloned.1.call-update) | async-done | bytes 524304 | tf_op jit(solution)/shard_map/reduce_scatter | solution.py:269
  395.9 2.6 convert_bitcast_fusion
  398.6 8.4 %all_gather.36 = bf16[1,256,1024]{2,1,0:T(8,128)(2,1)} all-gather(bf16[1,128,1024]{2,1,0:T(8,128)(2,1)S(1)} %get-tuple-element.301), channel_id=1, replica_groups=mesh['shard'=4,'ctx'=4,'tp'=2] {'tp'}, dimensions={1}, use_global_device_ids=true | all-gather | bytes 786432 | tf_op jit(solution)/shard_map/all_gather | solution.py:193
  407.4 17.9 %reduce-scatter.15.cloned.1.call-done = bf16[256,512]{0,1:T(8,128)(2,1)} async-done(((bf16[1024,512]{0,1:T(8,128)(2,1)}), bf16[256,512]{0,1:T(8,128)(2,1)}) %reduce-scatter.15.cloned.1.call-update) | async-done | bytes 262160 | tf_op jit(solution)/shard_map/reduce_scatter | solution.py:269
  425.3 39.4 %psum.7 = f32[12288]{0:T(1024)S(1)} all-reduce(f32[12288]{0:T(1024)S(1)} %constant_dynamic-update-slice_fusion), channel_id=1, replica_groups=mesh['shard'=4,'ctx'=4,'tp'=2] {'shard','ctx','tp'}, use_global_device_ids=true, to_apply=%region_28.29 | all-reduce | flops 12288 | bytes 98304 | tf_op jit(solution)/shard_map/psum | solution.py:286
  466.6 5.0 reshape.376
  471.6 4.6 slice_bitcast_fusion
  477.9 2.9 copy.47
  480.8 2.2 copy.56
  483.0 9.6 %reduce-scatter.13.cloned.1.call-done = bf16[1,128,1024]{2,1,0:T(8,128)(2,1)} async-done(((bf16[1,1024,1024]{2,1,0:T(8,128)(2,1)}), bf16[1,128,1024]{2,1,0:T(8,128)(2,1)}) %reduce-scatter.13.cloned.1.call-update) | async-done | bytes 262160 | tf_op jit(solution)/shard_map/reduce_scatter | solution.py:89
  493.6 8.7 %all_gather.39 = bf16[1,256,1024]{2,1,0:T(8,128)(2,1)} all-gather(bf16[1,128,1024]{2,1,0:T(8,128)(2,1)S(1)} %add_convert_fusion.1), channel_id=1, replica_groups=mesh['shard'=4,'ctx'=4,'tp'=2] {'tp'}, dimensions={1}, use_global_device_ids=true | all-gather | bytes 786432 | tf_op jit(solution)/shard_map/all_gather | solution.py:263
  502.3 8.6 %all-gather.17.cloned.1.call-done = bf16[1024,512]{0,1:T(8,128)(2,1)} async-done(((bf16[256,512]{0,1:T(8,128)(2,1)}), bf16[1024,512]{0,1:T(8,128)(2,1)}) %all-gather.17.cloned.1.call-update) | async-done | bytes 1048592 | tf_op jit(solution)/shard_map/all_gather | solution.py:270
  (199 shorter events, 68.7 us)
Async XLA Ops:
  7.2 92.1 %all-gather.9.cloned.1.call-start = ((), (), s32[]{:S(2)}) async-start(), calls=%async_computation.6 | async-start | bytes 2621440 | tf_op jit(solution)/shard_map/all_gather | solution.py:131
  9.7 16.4 %collective-permute-start = (bf16[1,256,1152]{2,1,0:T(8,128)(2,1)S(1)}, bf16[1,256,1152]{2,1,0:T(8,128)(2,1)S(1)}, u32[]{:S(2)}, u32[]{:S(2)}) collective-permute-start(bf16[1,256,1152]{2,1,0:T(8,128)(2,1)S(1)} %get-tuple-element.300), channel_id=1, source_target_pairs={{0,8},{8,0},{16,24},{24,16},{1,9},{9,1},{17,25},{25,17},{2,10},{10... | collective-permute-start | bytes 1769480 | tf_op jit(solution)/shard_map/ppermute | solution.py:22
  12.8 140.4 %reduce-scatter.7.cloned.1.call-start = ((), (), s32[]{:S(2)}) async-start(), calls=%async_computation.7 | async-start | bytes 2359296 | tf_op jit(solution)/shard_map/reduce_scatter | solution.py:89
  26.3 3.6 copy-start.11
  26.5 69.1 %collective-permute-start.1 = (bf16[2,256,1152]{2,1,0:T(8,128)(2,1)S(1)}, bf16[2,256,1152]{2,1,0:T(8,128)(2,1)}, u32[]{:S(2)}, u32[]{:S(2)}) collective-permute-start(bf16[2,256,1152]{2,1,0:T(8,128)(2,1)S(1)} %get-tuple-element.295), channel_id=1, source_target_pairs={{0,16},{8,24},{16,0},{24,8},{1,17},{9,25},{17,1},{25,9},{2,18},{10... | collective-permute-start | bytes 3538952 | tf_op jit(solution)/shard_map/ppermute | solution.py:22
  95.6 3.7 copy-start.8
  110.4 42.8 %copy-start.3 = (bf16[1,256,1024]{2,1,0:T(8,128)(2,1)S(1)}, bf16[1,256,1024]{2,1,0:T(8,128)(2,1)}, u32[]{:S(2)}) copy-start(bf16[1,256,1024]{2,1,0:T(8,128)(2,1)} %param.19) | copy-start | bytes 1572868
  110.5 42.8 %copy-start.12 = (f32[1024]{0:T(1024)S(1)}, f32[1024]{0:T(1024)}, u32[]{:S(2)}) copy-start(f32[1024]{0:T(1024)} %param.25) | copy-start | bytes 12292
  113.5 42.0 %copy-start.13 = (f32[1024]{0:T(1024)S(1)}, f32[1024]{0:T(1024)}, u32[]{:S(2)}) copy-start(f32[1024]{0:T(1024)} %param.26) | copy-start | bytes 12292
  113.5 42.0 %copy-start.14 = (f32[1024]{0:T(1024)S(1)}, f32[1024]{0:T(1024)}, u32[]{:S(2)}) copy-start(f32[1024]{0:T(1024)} %param.27) | copy-start | bytes 12292
  113.6 71.8 %all-gather.11.cloned.1.call-start = ((), (), s32[]{:S(2)}) async-start(), calls=%async_computation.8 | async-start | bytes 2359296 | tf_op jit(solution)/shard_map/all_gather | solution.py:85
  157.4 78.6 %reduce-scatter.9.cloned.1.call-start = ((), (), s32[]{:S(2)}) async-start(), calls=%async_computation.9 | async-start | bytes 2359296 | tf_op jit(solution)/shard_map/reduce_scatter | solution.py:89
  194.7 41.3 %copy-start.2 = (bf16[1,128,1024]{2,1,0:T(8,128)(2,1)S(1)}, bf16[1,128,1024]{2,1,0:T(8,128)(2,1)}, u32[]{:S(2)}) copy-start(bf16[1,128,1024]{2,1,0:T(8,128)(2,1)} %reduce-scatter.7.cloned.1.call-done) | copy-start | bytes 786436
  194.7 41.3 %copy-start.16 = (f32[1024]{0:T(1024)S(1)}, f32[1024]{0:T(1024)}, u32[]{:S(2)}) copy-start(f32[1024]{0:T(1024)} %param.31) | copy-start | bytes 12292
  194.7 42.8 %copy-start.10 = (bf16[1,256,1024]{2,1,0:T(8,128)(2,1)S(1)}, bf16[1,256,1024]{2,1,0:T(8,128)(2,1)}, u32[]{:S(2)}) copy-start(bf16[1,256,1024]{2,1,0:T(8,128)(2,1)} %param.20) | copy-start | bytes 1572868
  194.7 42.8 %copy-start.15 = (f32[1024]{0:T(1024)S(1)}, f32[1024]{0:T(1024)}, u32[]{:S(2)}) copy-start(f32[1024]{0:T(1024)} %param.32) | copy-start | bytes 12292
  194.7 43.1 %copy-start.17 = (f32[1024]{0:T(1024)S(1)}, f32[1024]{0:T(1024)}, u32[]{:S(2)}) copy-start(f32[1024]{0:T(1024)} %param.33) | copy-start | bytes 12292
  194.7 72.0 %all-gather.13.cloned.1.call-start = ((), (), s32[]{:S(2)}) async-start(), calls=%async_computation.10 | async-start | bytes 2359296 | tf_op jit(solution)/shard_map/all_gather | solution.py:85
  238.7 78.5 %reduce-scatter.11.cloned.1.call-start = ((), (), s32[]{:S(2)}) async-start(), calls=%async_computation.11 | async-start | bytes 2359296 | tf_op jit(solution)/shard_map/reduce_scatter | solution.py:89
  276.0 73.3 %all-gather.15.cloned.1.call-start = ((), (), s32[]{:S(2)}) async-start(), calls=%async_computation.12 | async-start | bytes 2359296 | tf_op jit(solution)/shard_map/all_gather | solution.py:85
  321.4 74.4 %reduce-scatter.17.cloned.1.call-start = ((), (), s32[]{:S(2)}) async-start(), calls=%async_computation.15 | async-start | bytes 2621440 | tf_op jit(solution)/shard_map/reduce_scatter | solution.py:269
  321.5 3.3 copy-start.19
  321.5 3.3 copy-start.22
  327.7 97.6 %reduce-scatter.15.cloned.1.call-start = ((), (), s32[]{:S(2)}) async-start(), calls=%async_computation.14 | async-start | bytes 1310720 | tf_op jit(solution)/shard_map/reduce_scatter | solution.py:269
  368.1 27.9 %copy-start.9 = (bf16[1024,384]{0,1:T(8,128)(2,1)S(1)}, bf16[1024,384]{0,1:T(8,128)(2,1)}, u32[]{:S(2)}) copy-start(bf16[1024,384]{0,1:T(8,128)(2,1)} %copy-done.8) | copy-start | bytes 2359300
  369.1 97.4 %all-gather.19.cloned.1.call-start = ((), (), s32[]{:S(2)}) async-start(), calls=%async_computation.17 | async-start | bytes 2621440 | tf_op jit(solution)/shard_map/all_gather | solution.py:270
  395.9 96.7 %reduce-scatter.13.cloned.1.call-start = ((), (), s32[]{:S(2)}) async-start(), calls=%async_computation.13 | async-start | bytes 2359296 | tf_op jit(solution)/shard_map/reduce_scatter | solution.py:89
  398.6 112.2 %all-gather.17.cloned.1.call-start = ((), (), s32[]{:S(2)}) async-start(), calls=%async_computation.16 | async-start | bytes 1310720 | tf_op jit(solution)/shard_map/all_gather | solution.py:270
  480.8 11.8 %copy-start.5 = (f32[1,128,1024]{2,1,0:T(8,128)S(1)}, f32[1,128,1024]{2,1,0:T(8,128)}, u32[]{:S(2)}) copy-start(f32[1,128,1024]{2,1,0:T(8,128)} %copy-done.4) | copy-start | bytes 1572868
  516.9 3.8 copy-start.6
  516.9 5.4 %copy-start.1 = (bf16[256,2048]{1,0:T(8,128)(2,1)S(1)}, bf16[256,2048]{1,0:T(8,128)(2,1)}, u32[]{:S(2)}) copy-start(bf16[256,2048]{1,0:T(8,128)(2,1)} %param.28) | copy-start | bytes 3145732
  518.7 2.8 copy-start.7
  (5 other events, 6.4 us)
Sparse Core Ops, SparseCore 0:
  13.0 22.7 all-gather.8
  113.7 39.5 reduce-scatter.6
  157.5 27.7 all-gather.10
  194.8 41.0 reduce-scatter.8
  238.9 27.7 all-gather.12
  276.1 41.0 reduce-scatter.10
  321.5 27.7 all-gather.14
  352.2 43.6 reduce-scatter.16
  398.7 26.4 reduce-scatter.14
  426.7 21.4 all-gather.18
  451.4 41.0 reduce-scatter.12
  494.0 16.8 all-gather.16
